TPU v7x, 32 devices: a whole 2x2x4 slice. The times are simulated.
32 devices in a mesh: rep: 4 (over y, x), fsdp: 2 (over core), tp: 4 (over z).
Axes of the slice: x: 2, y: 2, z: 4, core: 2. Of those that a mesh axis runs over, the one named last changes fastest.
Arguments:
- grad_parts: bfloat16 [2, 2, 8192, 1024], P('fsdp', None, 'rep', 'tp'), may hold values from -4 to 4
- master_weight: float32 [2, 8192, 1024], P(None, ('rep', 'fsdp'), 'tp'), may hold values from -0.0625 to 0.0625
- moment_one: float32 [2, 8192, 1024], P(None, ('rep', 'fsdp'), 'tp'), may hold values from -4 to 4
- moment_two: float32 [2, 8192, 1024], P(None, ('rep', 'fsdp'), 'tp'), may hold values from 0.1 to 2
- layer_inputs: bfloat16 [384, 4, 8192], P(('rep', 'fsdp'), None, 'tp'), may hold values from -6 to 6
- queries: bfloat16 [384, 4, 8192], P(('rep', 'fsdp'), None, 'tp'), may hold values from -105 to 105
- kv_cache: bfloat16 [384, 24, 2, 1024], P(('rep', 'fsdp'), None, None, 'tp'), may hold values from -4 to 4
- lengths: int32 [384], P(('rep', 'fsdp')), may hold values from 2 to 24
Outputs:
- new_master: float32 [2, 8192, 1024], P(None, ('rep', 'fsdp'), 'tp')
- new_moment_one: float32 [2, 8192, 1024], P(None, ('rep', 'fsdp'), 'tp')
- new_moment_two: float32 [2, 8192, 1024], P(None, ('rep', 'fsdp'), 'tp')
- context: bfloat16 [384, 4, 8192], P(('rep', 'fsdp'), None, 'tp')
Inputs may be any that keep to these rules, and one draw needn't show every extreme that they name: lengths[r] is the number of valid cached positions of row r, at most 24.
All inputs are finite; a program needn't handle non-finite values.
Results may differ from a plain program's by a relative error of at most 0.0065.
Values may be sent and summed in bfloat16 or wider, within the bound.
A program may use at most 64 MiB of HBM per device.

v0:
```python
import jax
import jax.numpy as jnp
from jax import lax
from jax.sharding import PartitionSpec as P

HD = 128


beta_one = 0.9
beta_two = 0.95
learning_rate = 0.001
weight_decay = 0.1
epsilon = 1e-08
first_bias = 1.0 - 0.9**10
second_bias = 1.0 - 0.95**10


def adamw_update(gradient, master, moment_one, moment_two):
    new_one = beta_one * moment_one + (1.0 - beta_one) * gradient
    new_two = beta_two * moment_two + (1.0 - beta_two) * gradient * gradient
    update = new_one / first_bias / (jnp.sqrt(new_two / second_bias) + epsilon)
    new_master = master - learning_rate * (update + weight_decay * master)
    return (new_one, new_two, new_master)


def attend(queries, kv_cache, fresh_keys, fresh_values, lengths):
    row_count = queries.shape[0]
    step_count = queries.shape[1]
    kv_heads = fresh_keys.shape[2]
    cache_len = kv_cache.shape[1]
    grouped = queries.reshape(row_count, step_count, kv_heads, -1, HD)
    cached_keys = kv_cache[:, :, 0].reshape(row_count, cache_len, kv_heads, HD)
    cached_values = kv_cache[:, :, 1].reshape(row_count, cache_len, kv_heads, HD)
    scaling = 1.0 / jnp.sqrt(jnp.float32(HD))
    cached_scores = (
        jnp.einsum("rsgqd,rcgd->rsgqc", grouped, cached_keys, preferred_element_type=jnp.float32)
        * scaling
    )
    fresh_scores = (
        jnp.einsum("rsgqd,rugd->rsgqu", grouped, fresh_keys, preferred_element_type=jnp.float32)
        * scaling
    )
    valid_old = jnp.arange(cache_len, dtype=jnp.int32)[None, :] < lengths[:, None]
    valid_old = valid_old[:, None, None, None, :]
    steps_index = jnp.arange(step_count, dtype=jnp.int32)
    valid_new = (steps_index[None, :] <= steps_index[:, None])[None, :, None, None, :]
    scores = jnp.concatenate(
        [
            jnp.where(valid_old, cached_scores, -jnp.inf),
            jnp.where(valid_new, fresh_scores, -jnp.inf),
        ],
        axis=-1,
    )
    row_max = jnp.max(scores, axis=-1, keepdims=True)
    exponent = jnp.exp(scores - row_max)
    weights = (exponent / jnp.sum(exponent, axis=-1, keepdims=True)).astype(jnp.bfloat16)
    output = jnp.einsum(
        "rsgqc,rcgd->rsgqd",
        weights[..., :cache_len],
        cached_values,
        preferred_element_type=jnp.float32,
    )
    output = output + jnp.einsum(
        "rsgqu,rugd->rsgqd",
        weights[..., cache_len:],
        fresh_values,
        preferred_element_type=jnp.float32,
    )
    return output.astype(jnp.bfloat16).reshape(row_count, step_count, -1)


def on_device(
    grad_parts, master_weight, moment_one, moment_two, layer_inputs, queries, kv_cache, lengths
):
    gradient = lax.psum_scatter(
        grad_parts[0].astype(jnp.float32).astype(jnp.bfloat16),
        "fsdp",
        scatter_dimension=1,
        tiled=True,
    ).astype(jnp.float32)
    new_one, new_two, new_master = adamw_update(gradient, master_weight, moment_one, moment_two)
    rollout_weight = new_master.astype(jnp.bfloat16)
    row_count = layer_inputs.shape[0]
    step_count = layer_inputs.shape[1]
    gathered = lax.all_gather(layer_inputs, "tp", axis=2, tiled=True)
    flattened = gathered.reshape(row_count * step_count, gathered.shape[2])
    projected = jnp.einsum(
        "td,kdc->ktc",
        flattened,
        lax.all_gather(rollout_weight, ("rep", "fsdp"), axis=1, tiled=True),
        preferred_element_type=jnp.float32,
    )
    fresh_pair = projected.astype(jnp.bfloat16).reshape(2, row_count, step_count, -1, HD)
    context = attend(queries, kv_cache, fresh_pair[0], fresh_pair[1], lengths)
    return (new_master, new_one, new_two, context)


def solution(mesh):
    return jax.shard_map(
        on_device,
        mesh=mesh,
        in_specs=(
            P("fsdp", None, "rep", "tp"),
            P(None, ("rep", "fsdp"), "tp"),
            P(None, ("rep", "fsdp"), "tp"),
            P(None, ("rep", "fsdp"), "tp"),
            P(("rep", "fsdp"), None, "tp"),
            P(("rep", "fsdp"), None, "tp"),
            P(("rep", "fsdp"), None, None, "tp"),
            P(("rep", "fsdp")),
        ),
        out_specs=(
            P(None, ("rep", "fsdp"), "tp"),
            P(None, ("rep", "fsdp"), "tp"),
            P(None, ("rep", "fsdp"), "tp"),
            P(("rep", "fsdp"), None, "tp"),
        ),
        check_vma=False,
    )
```

profile of v0, /device:TPU:0, one launch (start us, length us, event | category | flops | bytes accessed | tf_op | source)
XLA Modules:
  0.0 160.2 jit_solution(18076196282730567113)
XLA Ops:
  8.0 0.0 copy-start.2
  8.0 0.0 reduce-scatter.2.cloned.1.call-start
  8.1 0.7 reduce-scatter.2.cloned.1.call-update
  8.7 0.0 all-gather.5.cloned.1.call-start
  8.8 0.5 all-gather.5.cloned.1.call-update
  9.3 0.0 copy-start.3
  9.3 0.0 all-gather.3.cloned.1.call-start
  9.4 14.2 %reduce-scatter.2.cloned.1.call-done = bf16[2,1024,256]{2,1,0:T(8,128)(2,1)} async-done(((bf16[2,2048,256]{2,1,0:T(8,128)(2,1)}), bf16[2,1024,256]{2,1,0:T(8,128)(2,1)}) %reduce-scatter.2.cloned.1.call-update) | async-done | bytes 1048592 | tf_op jit(solution)/shard_map/reduce_scatter | solution.py:75
  23.6 0.0 copy-done.2
  23.6 6.7 %fusion.17 = (bf16[2,1024,256]{2,1,0:T(8,128)(2,1)}, f32[2,1024,256]{2,1,0:T(8,128)}, f32[2,1024,256]{2,1,0:T(8,128)}, f32[2,1024,256]{2,1,0:T(8,128)}) fusion(f32[2,1024,256]{2,1,0:T(8,128)S(1)} %copy-done.2, bf16[2,1024,256]{2,1,0:T(8,128)(2,1)} %reduce-scatter.2.cloned.1.call-done, f32[2,1024,256]{2,1,0:T(8,128)} %param.10, f32[2,1024,256]{2,1,0:T(8,128)} %param.11), kind=kLoop, calls=%fused_computation.30 | loop fusion | flops 8912896 | bytes 14680064 | tf_op jit(solution)/shard_map/convert_element_type | solution.py:82
  30.2 0.0 copy-start.1
  30.2 0.0 all-gather.3.cloned.1.call-update
  30.3 0.0 copy-done.3
  30.3 0.5 reshape.57
  30.8 0.7 copy-done.1
  31.5 0.0 copy-start.5
  31.5 4.9 %slice_reduce_fusion = (bf16[48,24,256]{2,1,0:T(8,128)(2,1)S(1)}, bf16[48,24,256]{2,1,0:T(8,128)(2,1)S(1)}) fusion(bf16[48,24,2,256]{3,2,1,0:T(2,128)(2,1)S(1)} %copy-done.1), kind=kLoop, calls=%fused_computation.11 | loop fusion | bytes 2359296 | tf_op jit(solution)/shard_map/slice | solution.py:33
  36.4 1.0 reshape_squeeze.6
  37.4 1.0 reshape_squeeze.7
  38.3 0.0 copy-done.5
  38.3 0.1 iota_compare_fusion
  38.4 1.7 %fusion.21 = (f32[48,4,2,8]{3,1,2,0:T(4,128)S(1)}, f32[48,4,2,8,24]{4,3,1,2,0:T(8,128)S(1)}) fusion(bf16[48,4,2,8,128]{4,3,2,1,0:T(8,128)(2,1)S(1)} %reshape.57, bf16[48,24,2,128,1]{3,2,1,0,4:T(2,128)(2,1)} %bitcast.23, pred[48,24]{1,0:T(8,128)(4,1)S(1)} %iota_compare_fusion), kind=kOutput, calls=%fused_computation.32 | convolution fusion | flops 19092480 | bytes 1684608 | tf_op jit(solution)/shard_map/rsgqd,rcgd->rsgqc/dot_general | solution.py:36
  40.1 36.7 %all-gather.5.cloned.1.call-done = bf16[48,4,8192]{2,1,0:T(4,128)(2,1)} async-done(((bf16[48,4,2048]{2,1,0:T(4,128)(2,1)}), bf16[48,4,8192]{2,1,0:T(4,128)(2,1)}) %all-gather.5.cloned.1.call-update) | async-done | bytes 3145744 | tf_op jit(solution)/shard_map/all_gather | solution.py:85
  76.9 5.5 %reshape.61 = bf16[192,8192,1]{1,0,2:T(8,128)(2,1)} reshape(bf16[48,4,8192]{2,1,0:T(4,128)(2,1)} %all-gather.5.cloned.1.call-done) | data formatting | bytes 6291456 | tf_op jit(solution)/shard_map/reshape | solution.py:86
  82.3 49.1 %all-gather.3.cloned.1.call-done = bf16[2,8192,256]{2,1,0:T(8,128)(2,1)} async-done(((bf16[2,1024,256]{2,1,0:T(8,128)(2,1)}), bf16[2,8192,256]{2,1,0:T(8,128)(2,1)}) %all-gather.3.cloned.1.call-update) | async-done | bytes 8388624 | tf_op jit(solution)/shard_map/all_gather | solution.py:90
  131.4 6.1 %fusion.4 = bf16[2,192,256]{2,1,0:T(8,128)(2,1)S(1)} fusion(bf16[192,8192,1]{1,0,2:T(8,128)(2,1)} %reshape.61, bf16[2,8192,256]{2,1,0:T(8,128)(2,1)} %all-gather.3.cloned.1.call-done), kind=kOutput, calls=%fused_computation.14 | convolution fusion | flops 1610711040 | bytes 11730944 | tf_op jit(solution)/shard_map/td,kdc->ktc/dot_general | solution.py:87
  137.6 0.6 fusion.20
  138.2 3.5 %fusion.8 = f32[48,2,4,4,8]{4,2,3,1,0:T(4,128)S(1)} fusion(bf16[48,4,2,8,128]{4,3,2,1,0:T(8,128)(2,1)S(1)} %reshape.57, bf16[48,4,2,128,1]{3,2,1,0,4:T(2,128)(2,1)S(1)} %bitcast.26), kind=kOutput, calls=%fused_computation.18 | convolution fusion | flops 3145728 | bytes 933888 | tf_op jit(solution)/shard_map/rsgqd,rugd->rsgqu/dot_general | solution.py:40
  141.8 0.5 copy.55
  142.3 0.7 fusion.16
  143.0 0.1 copy.57
  143.2 2.4 %copy.56 = f32[48,4,2,8,4]{4,3,1,2,0:T(8,128)S(1)} copy(f32[48,4,2,8,4]{0,3,1,4,2:T(8,128)} %get-tuple-element.23) | data formatting | bytes 98304 | tf_op jit(solution)/shard_map/jit(_where)/select_n | solution.py:50
  145.5 0.1 reduce_max.22
  145.6 1.5 fusion.13
  147.1 0.0 copy-start.4
  147.1 2.2 %divide_convert_fusion = bf16[48,4,2,8,28]{4,3,1,2,0:T(8,128)(2,1)} fusion(f32[48,4,2,8]{3,1,2,0:T(4,128)S(1)} %fusion.13, f32[48,4,2,8]{3,1,2,0:T(4,128)S(1)} %reduce_max.22, f32[48,4,2,8,4]{4,3,1,2,0:T(8,128)S(1)} %copy.56, f32[48,4,2,8,24]{4,3,1,2,0:T(8,128)S(1)} %get-tuple-element.31), kind=kLoop, calls=%fused_computation.9 | loop fusion | flops 344064 | bytes 540672 | tf_op jit(solution)/shard_map/convert_element_type | solution.py:56
  149.3 0.0 copy-start
  149.3 0.0 copy-done.4
  149.3 1.7 %fusion.6 = f32[48,2,4,8,128]{4,3,2,1,0:T(8,128)S(1)} fusion(bf16[48,4,2,8,28]{4,3,1,2,0:T(8,128)(2,1)} %divide_convert_fusion, bf16[48,24,2,128,1]{3,2,1,0,4:T(2,128)(2,1)} %bitcast.22), kind=kOutput, calls=%fused_computation.16 | convolution fusion | flops 18874368 | bytes 2334720 | tf_op jit(solution)/shard_map/rsgqc,rcgd->rsgqd/dot_general | solution.py:57
  151.1 0.0 copy-done
  151.1 0.4 fusion.3
  151.5 0.1 copy.76
  151.7 1.1 reshape.66
  (3 shorter events, 0.1 us)
Async XLA Ops:
  8.0 15.6 %copy-start.2 = (f32[2,1024,256]{2,1,0:T(8,128)S(1)}, f32[2,1024,256]{2,1,0:T(8,128)}, u32[]{:S(2)}) copy-start(f32[2,1024,256]{2,1,0:T(8,128)} %param.9) | copy-start | bytes 6291460
  8.0 15.6 %reduce-scatter.2.cloned.1.call-start = ((), (), s32[]{:S(2)}) async-start(), calls=%async_computation.1 | async-start | bytes 3145728 | tf_op jit(solution)/shard_map/reduce_scatter | solution.py:75
  8.7 68.1 %all-gather.5.cloned.1.call-start = ((), (), s32[]{:S(2)}) async-start(), calls=%async_computation.3 | async-start | bytes 3932160 | tf_op jit(solution)/shard_map/all_gather | solution.py:85
  9.3 20.9 %copy-start.3 = (bf16[48,4,2048]{2,1,0:T(4,128)(2,1)S(1)}, bf16[48,4,2048]{2,1,0:T(4,128)(2,1)}, u32[]{:S(2)}) copy-start(bf16[48,4,2048]{2,1,0:T(4,128)(2,1)} %param.13) | copy-start | bytes 2359300
  9.3 122.1 %all-gather.3.cloned.1.call-start = ((), (), s32[]{:S(2)}) async-start(), calls=%async_computation.2 | async-start | bytes 9437184 | tf_op jit(solution)/shard_map/all_gather | solution.py:90
  30.2 1.3 copy-start.1
  31.5 6.8 %copy-start.5 = (s32[48]{0:T(128)S(1)}, s32[48]{0:T(128)}, u32[]{:S(2)}) copy-start(s32[48]{0:T(128)} %param.15) | copy-start | bytes 580
  147.1 2.2 %copy-start.4 = (bf16[1,192,256]{2,1,0:T(8,128)(2,1)S(1)}, bf16[1,192,256]{2,1,0:T(8,128)(2,1)}, u32[]{:S(2)}) copy-start(bf16[1,192,256]{2,1,0:T(8,128)(2,1)} %get-tuple-element.28) | copy-start | bytes 294916
  149.3 1.8 %copy-start = (bf16[48,4,2,8,28]{4,3,1,2,0:T(8,128)(2,1)S(1)}, bf16[48,4,2,8,28]{4,3,1,2,0:T(8,128)(2,1)}, u32[]{:S(2)}) copy-start(bf16[48,4,2,8,28]{4,3,1,2,0:T(8,128)(2,1)} %divide_convert_fusion) | copy-start | bytes 516100
Sparse Core Ops, SparseCore 0:
  11.1 12.4 reduce-scatter.1
Sparse Core Ops, SparseCore 1:
  10.8 66.0 all-gather.4
  78.6 52.8 all-gather.2
where the time goes:
time: 161 us; the launch traced here: 160 us
  waiting for transfers between devices  101 us (63%)
  local copies, waits for them, and re-layouts  18.4 us (11%)
  between operations  15.6 us (10%)
  matrix products  13.6 us (8%)
  other arithmetic  11.2 us (7%)
    all_gather x1, waiting for transfers between devices, on_device(): lax.all_gather(rollout_weight, ('rep', 'fsdp'), axis=1, tiled=True)  49.1 us
    all_gather x1, waiting for transfers between devices, on_device(): gathered = lax.all_gather(layer_inputs, 'tp', axis=2, tiled=True)  36.7 us
    reduce_scatter x1, waiting for transfers between devices, on_device(): lax.psum_scatter(grad_parts[0].astype(jnp.float32).astype(jnp.bfloat16),...  14.2 us
    convert_element_type x1, other arithmetic, on_device(): rollout_weight = new_master.astype(jnp.bfloat16)  6.66 us
    dot_general x1, matrix products, on_device(): jnp.einsum('td,kdc->ktc', flattened, lax.all_gather(rollout_weight, ('rep...  6.13 us
    reshape x1, local copies, waits for them, and re-layouts, on_device(): flattened = gathered.reshape(row_count * step_count, gathered.shape[2])  5.49 us
    slice x1, local copies, waits for them, and re-layouts, attend(): kv_cache[:, :, 1].reshape(row_count, cache_len, kv_heads, HD)  4.9 us
    dot_general x1, matrix products, attend(): jnp.einsum('rsgqd,rugd->rsgqu', grouped, fresh_keys, preferred_element_ty...  3.54 us
  transfers between devices with their start and end apart: 3, of which 3 were waited for; matrix products, arithmetic and copies ran while one was open for 13% of the time, Pallas kernels for 0%

commit v1 on v0

--- a/solution.py
+++ b/solution.py
@@ -1,7 +1,391 @@
+import functools
+
 import jax
 import jax.numpy as jnp
 from jax import lax
+from jax.experimental import pallas as pl
+from jax.experimental.pallas import tpu as pltpu
 from jax.sharding import PartitionSpec as P
+
+MESH = pl.DeviceIdType.MESH
+W_CHUNKS = 4
+ADAM_SUB = 32
+TAIL_STEPS = 4
+
+
+def learner_kernel(
+    sizes, grad_hbm, master_hbm, one_hbm, two_hbm, x_hbm,
+    fresh_out, master_out, one_out, two_out,
+    own_grad, peer_grad, master, one, two, wbuf, xbuf, acc, partner_acc,
+    local_sem, out_sem, grad_send, grad_recv, x_send, x_recv, x_swap_send,
+    w_send, w_recv, w_fwd_send, acc_send, acc_recv,
+):
+    n_tp, depth = sizes
+    r, f, t = lax.axis_index("rep"), lax.axis_index("fsdp"), lax.axis_index("tp")
+    nf = 1 - f
+    rx = r + 1 - 2 * lax.rem(r, 2)
+    ry = lax.rem(r + 2, 4)
+    rd = lax.rem(rx + 2, 4)
+    partner, dev_x, dev_y = (r, nf, t), (rx, f, t), (ry, f, t)
+    up, down = (r, f, t + 1), (r, f, t - 1)
+    chunk = depth // W_CHUNKS
+
+    def half(index):
+        return pl.ds(pl.multiple_of(index * depth, depth), depth)
+
+    local = [
+        pltpu.make_async_copy(grad_hbm.at[0, :, half(f), :], own_grad, local_sem.at[0]),
+        pltpu.make_async_copy(master_hbm, master, local_sem.at[1]),
+        pltpu.make_async_copy(one_hbm, one, local_sem.at[2]),
+        pltpu.make_async_copy(two_hbm, two, local_sem.at[3]),
+        pltpu.make_async_copy(x_hbm.at[:, half(f)], xbuf.at[t, f], local_sem.at[4]),
+    ]
+    for copy in local:
+        copy.start()
+
+    barrier = pltpu.get_barrier_semaphore()
+    for device in (partner, dev_x, dev_y):
+        pl.semaphore_signal(barrier, inc=1, device_id=device, device_id_type=MESH)
+
+    @pl.when(t < n_tp - 1)
+    def _():
+        pl.semaphore_signal(barrier, inc=1, device_id=up, device_id_type=MESH)
+
+    @pl.when(t > 0)
+    def _():
+        pl.semaphore_signal(barrier, inc=1, device_id=down, device_id_type=MESH)
+
+    pl.semaphore_wait(barrier, jnp.where((t > 0) & (t < n_tp - 1), 5, 4))
+
+    def rows(c):
+        return pl.ds(pl.multiple_of(c * chunk, chunk), chunk)
+
+    def remote(src, dst, send, recv, device):
+        return pltpu.make_async_remote_copy(
+            src_ref=src, dst_ref=dst, send_sem=send, recv_sem=recv,
+            device_id=device, device_id_type=MESH,
+        )
+
+    def grad_copy(c):
+        source = pl.ds(pl.multiple_of(nf * depth + c * chunk, chunk), chunk)
+        return remote(
+            grad_hbm.at[0, :, source, :], peer_grad.at[:, rows(c), :],
+            grad_send.at[c], grad_recv.at[c], partner,
+        )
+
+    def x_move(z, th, side):
+        return remote(
+            xbuf.at[z, th], xbuf.at[z, th], x_send.at[side, z, th], x_recv.at[z, th],
+            up if side == 1 else down,
+        )
+
+    def x_own(side):
+        return remote(
+            x_hbm.at[:, half(f)], xbuf.at[t, f], x_send.at[side, t, f], x_recv.at[t, f],
+            up if side == 1 else down,
+        )
+
+    x_swap = remote(x_hbm.at[:, half(nf)], xbuf.at[t, f], x_swap_send.at[0], x_recv.at[t, f], partner)
+
+    def both_ways(act):
+        @pl.when(t < n_tp - 1)
+        def _():
+            act(1)
+
+        @pl.when(t > 0)
+        def _():
+            act(0)
+
+    grad_copy(0).start()
+    x_swap.start()
+    both_ways(lambda side: x_own(side).start())
+    for c in range(1, W_CHUNKS):
+        grad_copy(c).start()
+
+    def w_copy(c, way):
+        return remote(
+            wbuf.at[r, :, rows(c), :], wbuf.at[r, :, rows(c), :],
+            w_send.at[way, c], w_recv.at[r, c], dev_x if way == 0 else dev_y,
+        )
+
+    def w_arrived(owner, c):
+        remote(
+            wbuf.at[owner, :, rows(c), :], wbuf.at[owner, :, rows(c), :],
+            w_send.at[0, c], w_recv.at[owner, c], dev_x,
+        ).wait_recv()
+
+    def w_forward(c):
+        owner, device = (rx, dev_y) if c % 2 == 0 else (ry, dev_x)
+        return remote(
+            wbuf.at[owner, :, rows(c), :], wbuf.at[owner, :, rows(c), :],
+            w_fwd_send.at[c], w_recv.at[owner, c], device,
+        )
+
+    def x_arrived(z, th):
+        x_move(z, th, 1).wait_recv()
+
+    for copy in local[:4]:
+        copy.wait()
+
+    first_bias = 1.0 - 0.9**10
+    second_bias = 1.0 - 0.95**10
+
+    def adam(c):
+        def sub(i, carry):
+            at = pl.ds(pl.multiple_of(c * chunk + i * ADAM_SUB, ADAM_SUB), ADAM_SUB)
+            gradient = own_grad[:, at, :].astype(jnp.float32) + peer_grad[:, at, :].astype(jnp.float32)
+            new_one = 0.9 * one[:, at, :] + (1.0 - 0.9) * gradient
+            new_two = 0.95 * two[:, at, :] + (1.0 - 0.95) * gradient * gradient
+            update = new_one / first_bias / (jnp.sqrt(new_two / second_bias) + 1e-08)
+            old = master[:, at, :]
+            new_master = old - 0.001 * (update + 0.1 * old)
+            one[:, at, :] = new_one
+            two[:, at, :] = new_two
+            master[:, at, :] = new_master
+            wbuf[r, :, at, :] = new_master.astype(jnp.bfloat16)
+            return carry
+
+        lax.fori_loop(0, chunk // ADAM_SUB, sub, 0)
+
+    for c in range(W_CHUNKS):
+        grad_copy(c).wait_recv()
+        adam(c)
+        if c == 0:
+            x_arrived(t, nf)
+            both_ways(lambda side: x_move(t, nf, side).start())
+        else:
+            w_copy(c - 1, 0).start()
+            w_copy(c - 1, 1).start()
+    outs = [
+        pltpu.make_async_copy(master, master_out, out_sem.at[0]),
+        pltpu.make_async_copy(one, one_out, out_sem.at[1]),
+        pltpu.make_async_copy(two, two_out, out_sem.at[2]),
+    ]
+    for copy in outs:
+        copy.start()
+    w_copy(W_CHUNKS - 1, 0).start()
+    w_copy(W_CHUNKS - 1, 1).start()
+    local[4].wait()
+
+    def x_step(k, th):
+        @pl.when(t - k >= 0)
+        def _():
+            x_arrived(t - k, th)
+
+            @pl.when(t < n_tp - 1)
+            def _():
+                x_move(t - k, th, 1).start()
+
+        @pl.when(t + k < n_tp)
+        def _():
+            x_arrived(t + k, th)
+
+            @pl.when(t > 0)
+            def _():
+                x_move(t + k, th, 0).start()
+
+    def w_step(c):
+        w_arrived(rx, c)
+        w_arrived(ry, c)
+        w_forward(c).start()
+
+    x_step(1, f)
+    w_step(0)
+    x_step(1, nf)
+    w_step(1)
+    w_step(2)
+    x_step(2, f)
+    w_step(3)
+    x_step(2, nf)
+
+    acc[...] = jnp.zeros_like(acc)
+
+    def multiply(z, th):
+        def one_side(kv, carry):
+            acc[th, kv] += jnp.dot(xbuf[z, th], wbuf[z, kv], preferred_element_type=jnp.float32)
+            return carry
+
+        lax.fori_loop(0, 2, one_side, 0)
+
+    for c in range(W_CHUNKS):
+        w_arrived(rd, c)
+
+    def step(j, carry):
+        k = j // 2
+        th = f + lax.rem(j, 2) * (1 - 2 * f)
+
+        def side(s, inner):
+            z = t + (2 * s - 1) * k
+
+            @pl.when((z >= 0) & (z < n_tp))
+            def _():
+                @pl.when(k == n_tp - 1)
+                def _():
+                    x_arrived(z, th)
+
+                multiply(z, th)
+
+            return inner
+
+        lax.fori_loop(jnp.where(k == 0, 1, 0), 2, side, 0)
+        return carry
+
+    lax.fori_loop(0, 2 * n_tp, step, 0)
+
+    swap = remote(acc.at[nf], partner_acc, acc_send.at[0], acc_recv.at[0], partner)
+    swap.start()
+    for c in range(W_CHUNKS):
+        grad_copy(c).wait_send()
+        w_copy(c, 0).wait_send()
+        w_copy(c, 1).wait_send()
+        w_forward(c).wait_send()
+    x_swap.wait_send()
+    both_ways(lambda side: x_own(side).wait_send())
+    both_ways(lambda side: x_move(t, nf, side).wait_send())
+    for k in range(1, n_tp - 1):
+        for th in (f, nf):
+            @pl.when((t - k >= 0) & (t < n_tp - 1))
+            def _():
+                x_move(t - k, th, 1).wait_send()
+
+            @pl.when((t + k < n_tp) & (t > 0))
+            def _():
+                x_move(t + k, th, 0).wait_send()
+    for copy in outs:
+        copy.wait()
+    swap.wait_recv()
+    fresh_out[...] = (acc[f] + partner_acc[...]).astype(jnp.bfloat16)
+    swap.wait_send()
+
+
+def tail_kernel(
+    shape, lengths, q_ref, kv_ref, fresh_ref, master_in, one_in, two_in,
+    context, master_out, one_out, two_out,
+):
+    row_count, step_count, cache_len, head = shape
+    block = pl.program_id(0)
+    master_out[...] = master_in[...]
+    one_out[...] = one_in[...]
+    two_out[...] = two_in[...]
+    tokens = row_count * step_count
+    cached = row_count * cache_len
+    groups = fresh_ref.shape[2] // head
+    per_group = q_ref.shape[1] // head // groups
+    key_row = lax.broadcasted_iota(jnp.int32, (1, cached), 1) // cache_len
+    position = lax.broadcasted_iota(jnp.int32, (1, cached), 1) - key_row * cache_len
+    limit = jnp.zeros((1, cached), jnp.int32)
+    for row in range(row_count):
+        limit = jnp.where(key_row == row, lengths[block * row_count + row], limit)
+    key_row = jnp.where(position < limit, key_row, -1)
+    token = lax.broadcasted_iota(jnp.int32, (tokens, 1), 0)
+    old_ok = key_row == token // step_count
+    fresh = lax.broadcasted_iota(jnp.int32, (1, tokens), 1)
+    new_ok = (fresh // step_count == token // step_count) & (fresh <= token)
+    scale = head**-0.5
+    low = -0.7 * float(jnp.finfo(jnp.float32).max)
+    contract = (((1,), (1,)), ((), ()))
+    for group in range(groups):
+        cols = slice(group * head, (group + 1) * head)
+        vcols = slice((groups + group) * head, (groups + group + 1) * head)
+        query = jnp.concatenate(
+            [
+                q_ref[:, (group * per_group + h) * head : (group * per_group + h + 1) * head]
+                for h in range(per_group)
+            ],
+            axis=0,
+        )
+        old = lax.dot_general(query, kv_ref[:, cols], contract, preferred_element_type=jnp.float32)
+        new = lax.dot_general(query, fresh_ref[0, :, cols], contract, preferred_element_type=jnp.float32)
+        old = jnp.where(old_ok[None], old.reshape(per_group, tokens, cached) * scale, low)
+        new = jnp.where(new_ok[None], new.reshape(per_group, tokens, tokens) * scale, low)
+        top = jnp.maximum(jnp.max(old, axis=-1, keepdims=True), jnp.max(new, axis=-1, keepdims=True))
+        old = jnp.exp(old - top)
+        new = jnp.exp(new - top)
+        total = jnp.sum(old, axis=-1, keepdims=True) + jnp.sum(new, axis=-1, keepdims=True)
+        old = (old / total).astype(jnp.bfloat16).reshape(per_group * tokens, cached)
+        new = (new / total).astype(jnp.bfloat16).reshape(per_group * tokens, tokens)
+        out = jnp.dot(old, kv_ref[:, vcols], preferred_element_type=jnp.float32)
+        out = out + jnp.dot(new, fresh_ref[1, :, cols], preferred_element_type=jnp.float32)
+        out = out.astype(jnp.bfloat16)
+        for h in range(per_group):
+            at = (group * per_group + h) * head
+            context[:, at : at + head] = out[h * tokens : (h + 1) * tokens]
+
+
+def fused_device(head, n_rep, grad_parts, master_weight, moment_one, moment_two, layer_inputs, queries, kv_cache, lengths):
+    row_count, step_count, features = layer_inputs.shape
+    _, depth, width = master_weight.shape
+    n_tp = n_rep
+    tokens = row_count * step_count
+    cache_len = kv_cache.shape[1]
+    bf16, f32 = jnp.bfloat16, jnp.float32
+    dma = pltpu.SemaphoreType.DMA
+    state = jax.ShapeDtypeStruct(master_weight.shape, f32)
+    any_spec = pl.BlockSpec(memory_space=pl.ANY)
+    fresh, master, one, two = pl.pallas_call(
+        functools.partial(learner_kernel, (n_tp, depth)),
+        out_shape=(jax.ShapeDtypeStruct((2, tokens, width), bf16), state, state, state),
+        in_specs=[any_spec] * 5,
+        out_specs=(pl.BlockSpec(memory_space=pltpu.VMEM), any_spec, any_spec, any_spec),
+        scratch_shapes=[
+            pltpu.VMEM((2, depth, width), bf16),
+            pltpu.VMEM((2, depth, width), bf16),
+            pltpu.VMEM((2, depth, width), f32),
+            pltpu.VMEM((2, depth, width), f32),
+            pltpu.VMEM((2, depth, width), f32),
+            pltpu.VMEM((n_rep, 2, depth, width), bf16),
+            pltpu.VMEM((n_tp, 2, tokens, depth), bf16),
+            pltpu.VMEM((2, 2, tokens, width), f32),
+            pltpu.VMEM((2, tokens, width), f32),
+            dma((5,)),
+            dma((3,)),
+            dma((W_CHUNKS,)),
+            dma((W_CHUNKS,)),
+            dma((2, n_tp, 2)),
+            dma((n_tp, 2)),
+            dma((1,)),
+            dma((2, W_CHUNKS)),
+            dma((n_rep, W_CHUNKS)),
+            dma((W_CHUNKS,)),
+            dma((1,)),
+            dma((1,)),
+        ],
+        compiler_params=pltpu.CompilerParams(
+            collective_id=0, has_side_effects=True, vmem_limit_bytes=40 * 1024 * 1024
+        ),
+    )(grad_parts, master_weight, moment_one, moment_two, layer_inputs.reshape(tokens, features))
+    block_rows = row_count // TAIL_STEPS
+    block_tokens = tokens // TAIL_STEPS
+    state_spec = pl.BlockSpec((2, depth // TAIL_STEPS, width), lambda i, *_: (0, i, 0))
+    token_spec = pl.BlockSpec((block_tokens, features), lambda i, *_: (i, 0))
+    context, master, one, two = pl.pallas_call(
+        functools.partial(tail_kernel, (block_rows, step_count, cache_len, head)),
+        out_shape=(jax.ShapeDtypeStruct((tokens, features), bf16), state, state, state),
+        grid_spec=pltpu.PrefetchScalarGridSpec(
+            num_scalar_prefetch=1,
+            grid=(TAIL_STEPS,),
+            in_specs=[
+                token_spec,
+                pl.BlockSpec((block_rows * cache_len, 2 * width), lambda i, *_: (i, 0)),
+                pl.BlockSpec((2, block_tokens, width), lambda i, *_: (0, i, 0)),
+                state_spec,
+                state_spec,
+                state_spec,
+            ],
+            out_specs=(token_spec, state_spec, state_spec, state_spec),
+        ),
+        compiler_params=pltpu.CompilerParams(dimension_semantics=("arbitrary",)),
+    )(
+        lengths,
+        queries.reshape(tokens, features),
+        kv_cache.reshape(row_count * cache_len, 2 * width),
+        fresh,
+        master,
+        one,
+        two,
+    )
+    return (master, one, two, context.reshape(queries.shape))
+
 
 HD = 128
 
@@ -96,8 +480,11 @@
 
 
 def solution(mesh):
+    shape = mesh.shape
+    fits = shape["rep"] == 4 and shape["tp"] == 4 and shape["fsdp"] == 2
+    run = functools.partial(fused_device, HD, shape["rep"]) if fits else on_device
     return jax.shard_map(
-        on_device,
+        run,
         mesh=mesh,
         in_specs=(
             P("fsdp", None, "rep", "tp"),

time: 161 us -> 86.1 us (0.53)
  waiting for transfers between devices: 101 us -> 0 us
  Pallas kernels: 0 us -> 68.3 us
  between operations: 15.6 us -> 0.67 us
  matrix products: 13.6 us -> 0 us
  other arithmetic: 11.2 us -> 0 us
  local copies, waits for them, and re-layouts: 18.4 us -> 16.7 us
    all_gather x2 -> x0, waiting for transfers between devices: 85.8 us -> none  [the longest x1 49.1 us: on_device(): lax.all_gather(rollout_weight, ('rep', 'fsdp'), axis=1, tiled=True)]
    pallas_call x0 -> x2, Pallas kernels: none -> 68.3 us  [the longest x1 58.6 us: fused_device(): pl.pallas_call(functools.partial(learner_kernel, (n_tp, depth)), out_shap...]
    reduce_scatter x1 -> x0, waiting for transfers between devices: 14.2 us -> none  [on_device(): lax.psum_scatter(grad_parts[0].astype(jnp.float32).astype(jnp.bfloat16),...]
    dot_general x5 -> x0, matrix products: 13.6 us -> none  [the longest x1 6.13 us: on_device(): jnp.einsum('td,kdc->ktc', flattened, lax.all_gather(rollout_weight, ('rep...]
    convert_element_type x2 -> x0, other arithmetic: 8.84 us -> none  [the longest x1 6.66 us: on_device(): rollout_weight = new_master.astype(jnp.bfloat16)]
    unnamed x14 -> x15, local copies, waits for them, and re-layouts: 1.95 us -> 10.4 us
    slice x2 -> x0, local copies, waits for them, and re-layouts: 5.54 us -> none  [the longest x1 4.9 us: attend(): kv_cache[:, :, 1].reshape(row_count, cache_len, kv_heads, HD)]
    select_n x1 -> x0, local copies, waits for them, and re-layouts: 2.36 us -> none  [attend(): jnp.where(valid_new, fresh_scores, -jnp.inf)]
  transfers between devices with their start and end apart: 3 -> 0, of which waited for: 3 -> 0; matrix products, arithmetic and copies ran while one was open for 13% -> 0% of each run, Pallas kernels for 0% -> 0%
where the time goes in v1:
time: 86.1 us; the launch traced here: 85.7 us
  Pallas kernels  68.3 us (79%)
  local copies, waits for them, and re-layouts  16.7 us (19%)
    pallas_call x1, Pallas kernels, fused_device(): pl.pallas_call(functools.partial(learner_kernel, (n_tp, depth)), out_shap...  58.6 us
    unnamed x15, local copies, waits for them, and re-layouts  10.4 us
    pallas_call x1, Pallas kernels, fused_device(): pl.pallas_call(functools.partial(tail_kernel, (block_rows, step_count, ca...  9.77 us
    reshape x1, local copies, waits for them, and re-layouts, fused_device(): queries.reshape(tokens, features)  2.41 us
    reshape x1, local copies, waits for them, and re-layouts, fused_device(): return (master, one, two, context.reshape(queries.shape))  2.37 us

profile of v1, /device:TPU:0, one launch (start us, length us, event | category | flops | bytes accessed | tf_op | source)
XLA Modules:
  0.0 85.7 jit_solution(11675852490749719330)
XLA Ops:
  0.6 1.6 %reshape.22.x_hbm = bf16[192,2048]{1,0:T(8,128)(2,1)S(1)} reshape(bf16[48,4,2048]{2,1,0:T(4,128)(2,1)} %param.12) | data formatting | bytes 1572864 | tf_op jit(solution)/shard_map/reshape | solution.py:356
  2.2 0.0 copy-start
  2.2 2.4 %reshape.20.q_ref = bf16[192,2048]{1,0:T(8,128)(2,1)} reshape(bf16[48,4,2048]{2,1,0:T(4,128)(2,1)} %param.13) | data formatting | bytes 1572864 | tf_op jit(solution)/shard_map/reshape | solution.py:380
  4.6 2.6 %copy.12 = bf16[144,8,2,256]{3,1,2,0:T(8,128)(2,1)} copy(bf16[144,8,2,256]{3,2,1,0:T(2,128)(2,1)} %bitcast.4) | data formatting | bytes 2359296
  7.2 0.0 copy-done
  7.2 0.0 copy-start.1
  7.2 1.6 %copy-done.1 = f32[2,1024,256]{2,1,0:T(8,128)S(1)} copy-done((f32[2,1024,256]{2,1,0:T(8,128)S(1)}, f32[2,1024,256]{2,1,0:T(8,128)}, u32[]{:S(2)}) %copy-start.1) | copy-done | bytes 2097176
  8.8 0.0 copy-start.2
  8.8 1.6 %copy-done.2 = f32[2,1024,256]{2,1,0:T(8,128)S(1)} copy-done((f32[2,1024,256]{2,1,0:T(8,128)S(1)}, f32[2,1024,256]{2,1,0:T(8,128)}, u32[]{:S(2)}) %copy-start.2) | copy-done | bytes 2097176
  10.4 58.6 %shard_map.111 = (bf16[2,192,256]{2,1,0:T(8,128)(2,1)S(1)}, f32[2,1024,256]{2,1,0:T(8,128)S(1)}, f32[2,1024,256]{2,1,0:T(8,128)S(1)}, f32[2,1024,256]{2,1,0:T(8,128)S(1)}) custom-call(bf16[1,2,2048,256]{3,2,1,0:T(8,128)(2,1)S(1)} %copy-done, f32[2,1024,256]{2,1,0:T(8,128)S(1)} %copy-done.1, f32[2,1024,256]{2,1,0:T(8,128)S(1)} %copy-done.2, ...), custom_call_target="tpu_custom_call" | custom-call | tf_op jit(solution)/shard_map/pallas_call | solution.py:325
  68.9 0.0 copy-start.3
  68.9 1.3 %copy-done.3 = f32[2,1024,256]{2,1,0:T(8,128)} copy-done((f32[2,1024,256]{2,1,0:T(8,128)}, f32[2,1024,256]{2,1,0:T(8,128)S(1)}, u32[]{:S(2)}) %copy-start.3) | copy-done | bytes 2097176
  70.3 0.0 copy-start.4
  70.3 1.3 %copy-done.4 = f32[2,1024,256]{2,1,0:T(8,128)} copy-done((f32[2,1024,256]{2,1,0:T(8,128)}, f32[2,1024,256]{2,1,0:T(8,128)S(1)}, u32[]{:S(2)}) %copy-start.4) | copy-done | bytes 2097176
  71.6 0.0 copy-start.5
  71.6 1.3 %copy-done.5 = f32[2,1024,256]{2,1,0:T(8,128)} copy-done((f32[2,1024,256]{2,1,0:T(8,128)}, f32[2,1024,256]{2,1,0:T(8,128)S(1)}, u32[]{:S(2)}) %copy-start.5) | copy-done | bytes 2097176
  72.9 0.0 copy-start.6
  72.9 0.7 copy-done.6
  73.6 9.8 %shard_map.112 = (bf16[192,2048]{1,0:T(8,128)(2,1)}, f32[2,1024,256]{2,1,0:T(8,128)}, f32[2,1024,256]{2,1,0:T(8,128)}, f32[2,1024,256]{2,1,0:T(8,128)}) custom-call(s32[48]{0:T(128)} %lengths.1, bf16[192,2048]{1,0:T(8,128)(2,1)} %reshape.20.q_ref, bf16[1152,512]{1,0:T(8,128)(2,1)} %bitcast.3, bf16[2,192,256]{2,1,0:T(8,128)(2,1)} %copy-done.6, ...), custom_call_target="tpu_custom_call" | custom-call | tf_op jit(solution)/shard_map/pallas_call | solution.py:361
  83.4 2.4 %reshape.23 = bf16[48,4,2048]{2,1,0:T(4,128)(2,1)} reshape(bf16[192,2048]{1,0:T(8,128)(2,1)} %get-tuple-element.19) | data formatting | bytes 1572864 | tf_op jit(solution)/shard_map/reshape | solution.py:387
Async XLA Ops:
  2.2 5.0 %copy-start = (bf16[1,2,2048,256]{3,2,1,0:T(8,128)(2,1)S(1)}, bf16[1,2,2048,256]{3,2,1,0:T(8,128)(2,1)}, u32[]{:S(2)}) copy-start(bf16[1,2,2048,256]{3,2,1,0:T(8,128)(2,1)} %grad_hbm.1) | copy-start | bytes 6291460
  7.2 1.6 %copy-start.1 = (f32[2,1024,256]{2,1,0:T(8,128)S(1)}, f32[2,1024,256]{2,1,0:T(8,128)}, u32[]{:S(2)}) copy-start(f32[2,1024,256]{2,1,0:T(8,128)} %master_hbm.1) | copy-start | bytes 6291460
  8.8 1.6 %copy-start.2 = (f32[2,1024,256]{2,1,0:T(8,128)S(1)}, f32[2,1024,256]{2,1,0:T(8,128)}, u32[]{:S(2)}) copy-start(f32[2,1024,256]{2,1,0:T(8,128)} %one_hbm.1) | copy-start | bytes 6291460
  68.9 1.3 %copy-start.3 = (f32[2,1024,256]{2,1,0:T(8,128)}, f32[2,1024,256]{2,1,0:T(8,128)S(1)}, u32[]{:S(2)}) copy-start(f32[2,1024,256]{2,1,0:T(8,128)S(1)} %get-tuple-element.13.master_in) | copy-start | bytes 6291460
  70.3 1.3 %copy-start.4 = (f32[2,1024,256]{2,1,0:T(8,128)}, f32[2,1024,256]{2,1,0:T(8,128)S(1)}, u32[]{:S(2)}) copy-start(f32[2,1024,256]{2,1,0:T(8,128)S(1)} %get-tuple-element.14.one_in) | copy-start | bytes 6291460
  71.6 1.3 %copy-start.5 = (f32[2,1024,256]{2,1,0:T(8,128)}, f32[2,1024,256]{2,1,0:T(8,128)S(1)}, u32[]{:S(2)}) copy-start(f32[2,1024,256]{2,1,0:T(8,128)S(1)} %get-tuple-element.15.two_in) | copy-start | bytes 6291460
  72.9 0.7 copy-start.6

commit v2 on v1

--- a/solution.py
+++ b/solution.py
@@ -7,16 +7,17 @@
 from jax.experimental.pallas import tpu as pltpu
 from jax.sharding import PartitionSpec as P
 
+HD = 128
 MESH = pl.DeviceIdType.MESH
 W_CHUNKS = 4
 ADAM_SUB = 32
-TAIL_STEPS = 4
+TAIL_ROWS = 8
 
 
 def learner_kernel(
-    sizes, grad_hbm, master_hbm, one_hbm, two_hbm, x_hbm,
-    fresh_out, master_out, one_out, two_out,
-    own_grad, peer_grad, master, one, two, wbuf, xbuf, acc, partner_acc,
+    sizes, grad_hbm, master_hbm, one_hbm, two_hbm, x_hbm, kv_hbm,
+    fresh_out, cached_out, master_out, one_out, two_out,
+    own_grad, peer_grad, master, one, two, wbuf, xbuf, xflat, acc, partner_acc, kv_raw, kv_flat,
     local_sem, out_sem, grad_send, grad_recv, x_send, x_recv, x_swap_send,
     w_send, w_recv, w_fwd_send, acc_send, acc_recv,
 ):
@@ -38,7 +39,8 @@
         pltpu.make_async_copy(master_hbm, master, local_sem.at[1]),
         pltpu.make_async_copy(one_hbm, one, local_sem.at[2]),
         pltpu.make_async_copy(two_hbm, two, local_sem.at[3]),
-        pltpu.make_async_copy(x_hbm.at[:, half(f)], xbuf.at[t, f], local_sem.at[4]),
+        pltpu.make_async_copy(x_hbm.at[:, :, half(f)], xbuf.at[t, f], local_sem.at[4]),
+        pltpu.make_async_copy(kv_hbm, kv_raw, local_sem.at[5]),
     ]
     for copy in local:
         copy.start()
@@ -81,11 +83,11 @@
 
     def x_own(side):
         return remote(
-            x_hbm.at[:, half(f)], xbuf.at[t, f], x_send.at[side, t, f], x_recv.at[t, f],
+            x_hbm.at[:, :, half(f)], xbuf.at[t, f], x_send.at[side, t, f], x_recv.at[t, f],
             up if side == 1 else down,
         )
 
-    x_swap = remote(x_hbm.at[:, half(nf)], xbuf.at[t, f], x_swap_send.at[0], x_recv.at[t, f], partner)
+    x_swap = remote(x_hbm.at[:, :, half(nf)], xbuf.at[t, f], x_swap_send.at[0], x_recv.at[t, f], partner)
 
     def both_ways(act):
         @pl.when(t < n_tp - 1)
@@ -166,6 +168,7 @@
     w_copy(W_CHUNKS - 1, 0).start()
     w_copy(W_CHUNKS - 1, 1).start()
     local[4].wait()
+    local[5].wait()
 
     def x_step(k, th):
         @pl.when(t - k >= 0)
@@ -189,9 +192,28 @@
         w_arrived(ry, c)
         w_forward(c).start()
 
+    kv_rows, cache_len = kv_raw.shape[:2]
+    pieces = kv_rows // 8
+
+    def split_cache(quarter):
+        def body(i, carry):
+            row = (quarter * pieces + i) * 2
+            at = pl.ds(pl.multiple_of(row * cache_len, 2 * cache_len), 2 * cache_len)
+            for j in range(2):
+                kv_flat[j, at, :] = kv_raw[pl.ds(row, 2), :, j, :].reshape(2 * cache_len, -1)
+            return carry
+
+        lax.fori_loop(0, pieces, body, 0)
+
+    split_cache(0)
     x_step(1, f)
+    split_cache(1)
     w_step(0)
+    split_cache(2)
     x_step(1, nf)
+    split_cache(3)
+    cached_copy = pltpu.make_async_copy(kv_flat, cached_out, out_sem.at[3])
+    cached_copy.start()
     w_step(1)
     w_step(2)
     x_step(2, f)
@@ -200,9 +222,20 @@
 
     acc[...] = jnp.zeros_like(acc)
 
+    x_rows = xbuf.shape[2]
+    x_part = x_rows // 4
+    flat_part = xflat.shape[0] // 4
+
     def multiply(z, th):
+        def flatten(i, carry):
+            at = pl.ds(pl.multiple_of(i * flat_part, flat_part), flat_part)
+            xflat[at, :] = xbuf[z, th, pl.ds(i * x_part, x_part)].reshape(flat_part, depth)
+            return carry
+
+        lax.fori_loop(0, 4, flatten, 0)
+
         def one_side(kv, carry):
-            acc[th, kv] += jnp.dot(xbuf[z, th], wbuf[z, kv], preferred_element_type=jnp.float32)
+            acc[th, kv] += jnp.dot(xflat[...], wbuf[z, kv], preferred_element_type=jnp.float32)
             return carry
 
         lax.fori_loop(0, 2, one_side, 0)
@@ -253,66 +286,84 @@
                 x_move(t + k, th, 0).wait_send()
     for copy in outs:
         copy.wait()
+    cached_copy.wait()
     swap.wait_recv()
     fresh_out[...] = (acc[f] + partner_acc[...]).astype(jnp.bfloat16)
     swap.wait_send()
 
 
 def tail_kernel(
-    shape, lengths, q_ref, kv_ref, fresh_ref, master_in, one_in, two_in,
-    context, master_out, one_out, two_out,
+    lengths, q_ref, kv_ref, fresh_in, master_in, one_in, two_in,
+    context, master_out, one_out, two_out, fresh_ref, sem,
 ):
-    row_count, step_count, cache_len, head = shape
     block = pl.program_id(0)
-    master_out[...] = master_in[...]
-    one_out[...] = one_in[...]
-    two_out[...] = two_in[...]
+    moves = [
+        pltpu.make_async_copy(master_in, master_out, sem.at[1]),
+        pltpu.make_async_copy(one_in, one_out, sem.at[2]),
+        pltpu.make_async_copy(two_in, two_out, sem.at[3]),
+    ]
+
+    @pl.when(block == 0)
+    def _():
+        fresh_copy = pltpu.make_async_copy(fresh_in, fresh_ref, sem.at[0])
+        fresh_copy.start()
+        for move in moves:
+            move.start()
+        fresh_copy.wait()
+
+    row_count, step_count, features = q_ref.shape
+    cached = kv_ref.shape[1]
+    head = HD
+    cache_len = cached // row_count
     tokens = row_count * step_count
-    cached = row_count * cache_len
+    keys = cached + tokens
     groups = fresh_ref.shape[2] // head
-    per_group = q_ref.shape[1] // head // groups
-    key_row = lax.broadcasted_iota(jnp.int32, (1, cached), 1) // cache_len
-    position = lax.broadcasted_iota(jnp.int32, (1, cached), 1) - key_row * cache_len
-    limit = jnp.zeros((1, cached), jnp.int32)
+    per_group = features // head // groups
+    here = pl.ds(pl.multiple_of(block * tokens, tokens), tokens)
+    column = lax.broadcasted_iota(jnp.int32, (1, keys), 1)
+    is_old = column < cached
+    new_column = column - cached
+    key_row = jnp.where(is_old, column // cache_len, new_column // step_count)
+    position = column - key_row * cache_len
+    limit = jnp.zeros((1, keys), jnp.int32)
     for row in range(row_count):
         limit = jnp.where(key_row == row, lengths[block * row_count + row], limit)
-    key_row = jnp.where(position < limit, key_row, -1)
+    old_row = jnp.where(is_old & (position < limit), key_row, -1)
+    new_row = jnp.where(is_old, -1, key_row)
     token = lax.broadcasted_iota(jnp.int32, (tokens, 1), 0)
-    old_ok = key_row == token // step_count
-    fresh = lax.broadcasted_iota(jnp.int32, (1, tokens), 1)
-    new_ok = (fresh // step_count == token // step_count) & (fresh <= token)
-    scale = head**-0.5
+    row = token // step_count
+    valid = (old_row == row) | ((new_row == row) & (new_column <= token))
     low = -0.7 * float(jnp.finfo(jnp.float32).max)
     contract = (((1,), (1,)), ((), ()))
     for group in range(groups):
         cols = slice(group * head, (group + 1) * head)
-        vcols = slice((groups + group) * head, (groups + group + 1) * head)
         query = jnp.concatenate(
             [
-                q_ref[:, (group * per_group + h) * head : (group * per_group + h + 1) * head]
+                q_ref[:, :, (group * per_group + h) * head : (group * per_group + h + 1) * head].reshape(tokens, head)
                 for h in range(per_group)
             ],
             axis=0,
         )
-        old = lax.dot_general(query, kv_ref[:, cols], contract, preferred_element_type=jnp.float32)
-        new = lax.dot_general(query, fresh_ref[0, :, cols], contract, preferred_element_type=jnp.float32)
-        old = jnp.where(old_ok[None], old.reshape(per_group, tokens, cached) * scale, low)
-        new = jnp.where(new_ok[None], new.reshape(per_group, tokens, tokens) * scale, low)
-        top = jnp.maximum(jnp.max(old, axis=-1, keepdims=True), jnp.max(new, axis=-1, keepdims=True))
-        old = jnp.exp(old - top)
-        new = jnp.exp(new - top)
-        total = jnp.sum(old, axis=-1, keepdims=True) + jnp.sum(new, axis=-1, keepdims=True)
-        old = (old / total).astype(jnp.bfloat16).reshape(per_group * tokens, cached)
-        new = (new / total).astype(jnp.bfloat16).reshape(per_group * tokens, tokens)
-        out = jnp.dot(old, kv_ref[:, vcols], preferred_element_type=jnp.float32)
-        out = out + jnp.dot(new, fresh_ref[1, :, cols], preferred_element_type=jnp.float32)
-        out = out.astype(jnp.bfloat16)
+        key = jnp.concatenate([kv_ref[0, :, cols], fresh_ref[0, here, cols]], axis=0)
+        value = jnp.concatenate([kv_ref[1, :, cols], fresh_ref[1, here, cols]], axis=0)
+        scores = lax.dot_general(query, key, contract, preferred_element_type=jnp.float32)
+        scores = jnp.where(valid[None], scores.reshape(per_group, tokens, keys) * head**-0.5, low)
+        weights = jnp.exp(scores - jnp.max(scores, axis=-1, keepdims=True))
+        weights = weights * (1.0 / jnp.sum(weights, axis=-1, keepdims=True))
+        weights = weights.astype(jnp.bfloat16).reshape(per_group * tokens, keys)
+        out = jnp.dot(weights, value, preferred_element_type=jnp.float32)
         for h in range(per_group):
             at = (group * per_group + h) * head
-            context[:, at : at + head] = out[h * tokens : (h + 1) * tokens]
-
-
-def fused_device(head, n_rep, grad_parts, master_weight, moment_one, moment_two, layer_inputs, queries, kv_cache, lengths):
+            piece = out[h * tokens : (h + 1) * tokens].reshape(row_count, step_count, head)
+            context[:, :, at : at + head] = piece.astype(jnp.bfloat16)
+
+    @pl.when(block == pl.num_programs(0) - 1)
+    def _():
+        for move in moves:
+            move.wait()
+
+
+def fused_device(n_rep, grad_parts, master_weight, moment_one, moment_two, layer_inputs, queries, kv_cache, lengths):
     row_count, step_count, features = layer_inputs.shape
     _, depth, width = master_weight.shape
     n_tp = n_rep
@@ -322,11 +373,18 @@
     dma = pltpu.SemaphoreType.DMA
     state = jax.ShapeDtypeStruct(master_weight.shape, f32)
     any_spec = pl.BlockSpec(memory_space=pl.ANY)
-    fresh, master, one, two = pl.pallas_call(
+    hbm_spec = pl.BlockSpec(memory_space=pltpu.HBM)
+    fresh, cached, master, one, two = pl.pallas_call(
         functools.partial(learner_kernel, (n_tp, depth)),
-        out_shape=(jax.ShapeDtypeStruct((2, tokens, width), bf16), state, state, state),
-        in_specs=[any_spec] * 5,
-        out_specs=(pl.BlockSpec(memory_space=pltpu.VMEM), any_spec, any_spec, any_spec),
+        out_shape=(
+            jax.ShapeDtypeStruct((2, tokens, width), bf16),
+            jax.ShapeDtypeStruct((2, row_count * cache_len, width), bf16),
+            state,
+            state,
+            state,
+        ),
+        in_specs=[hbm_spec] * 6,
+        out_specs=(pl.BlockSpec(memory_space=pltpu.VMEM), hbm_spec, any_spec, any_spec, any_spec),
         scratch_shapes=[
             pltpu.VMEM((2, depth, width), bf16),
             pltpu.VMEM((2, depth, width), bf16),
@@ -334,11 +392,14 @@
             pltpu.VMEM((2, depth, width), f32),
             pltpu.VMEM((2, depth, width), f32),
             pltpu.VMEM((n_rep, 2, depth, width), bf16),
-            pltpu.VMEM((n_tp, 2, tokens, depth), bf16),
+            pltpu.VMEM((n_tp, 2, row_count, step_count, depth), bf16),
+            pltpu.VMEM((tokens, depth), bf16),
             pltpu.VMEM((2, 2, tokens, width), f32),
             pltpu.VMEM((2, tokens, width), f32),
-            dma((5,)),
-            dma((3,)),
+            pltpu.VMEM(kv_cache.shape, bf16),
+            pltpu.VMEM((2, row_count * cache_len, width), bf16),
+            dma((6,)),
+            dma((4,)),
             dma((W_CHUNKS,)),
             dma((W_CHUNKS,)),
             dma((2, n_tp, 2)),
@@ -351,43 +412,32 @@
             dma((1,)),
         ],
         compiler_params=pltpu.CompilerParams(
-            collective_id=0, has_side_effects=True, vmem_limit_bytes=40 * 1024 * 1024
+            collective_id=0, has_side_effects=True, vmem_limit_bytes=36 * 1024 * 1024
         ),
-    )(grad_parts, master_weight, moment_one, moment_two, layer_inputs.reshape(tokens, features))
-    block_rows = row_count // TAIL_STEPS
-    block_tokens = tokens // TAIL_STEPS
-    state_spec = pl.BlockSpec((2, depth // TAIL_STEPS, width), lambda i, *_: (0, i, 0))
-    token_spec = pl.BlockSpec((block_tokens, features), lambda i, *_: (i, 0))
+    )(grad_parts, master_weight, moment_one, moment_two, layer_inputs, kv_cache)
+    token_spec = pl.BlockSpec((TAIL_ROWS, step_count, features), lambda i, *_: (i, 0, 0))
     context, master, one, two = pl.pallas_call(
-        functools.partial(tail_kernel, (block_rows, step_count, cache_len, head)),
-        out_shape=(jax.ShapeDtypeStruct((tokens, features), bf16), state, state, state),
+        tail_kernel,
+        out_shape=(jax.ShapeDtypeStruct(queries.shape, bf16), state, state, state),
         grid_spec=pltpu.PrefetchScalarGridSpec(
             num_scalar_prefetch=1,
-            grid=(TAIL_STEPS,),
+            grid=(row_count // TAIL_ROWS,),
             in_specs=[
                 token_spec,
-                pl.BlockSpec((block_rows * cache_len, 2 * width), lambda i, *_: (i, 0)),
-                pl.BlockSpec((2, block_tokens, width), lambda i, *_: (0, i, 0)),
-                state_spec,
-                state_spec,
-                state_spec,
+                pl.BlockSpec((2, TAIL_ROWS * cache_len, width), lambda i, *_: (0, i, 0)),
+                any_spec,
+                any_spec,
+                any_spec,
+                any_spec,
             ],
-            out_specs=(token_spec, state_spec, state_spec, state_spec),
+            out_specs=(token_spec, hbm_spec, hbm_spec, hbm_spec),
+            scratch_shapes=[pltpu.VMEM((2, tokens, width), bf16), dma((4,))],
         ),
-        compiler_params=pltpu.CompilerParams(dimension_semantics=("arbitrary",)),
-    )(
-        lengths,
-        queries.reshape(tokens, features),
-        kv_cache.reshape(row_count * cache_len, 2 * width),
-        fresh,
-        master,
-        one,
-        two,
-    )
-    return (master, one, two, context.reshape(queries.shape))
-
-
-HD = 128
+        compiler_params=pltpu.CompilerParams(
+            dimension_semantics=("arbitrary",), vmem_limit_bytes=16 * 1024 * 1024
+        ),
+    )(lengths, queries, cached, fresh, master, one, two)
+    return (master, one, two, context)
 
 
 beta_one = 0.9
@@ -482,7 +532,7 @@
 def solution(mesh):
     shape = mesh.shape
     fits = shape["rep"] == 4 and shape["tp"] == 4 and shape["fsdp"] == 2
-    run = functools.partial(fused_device, HD, shape["rep"]) if fits else on_device
+    run = functools.partial(fused_device, shape["rep"]) if fits else on_device
     return jax.shard_map(
         run,
         mesh=mesh,

time: 86.1 us -> 76.9 us (0.89)
  local copies, waits for them, and re-layouts: 16.7 us -> 8.77 us
  Pallas kernels: 68.3 us -> 67.1 us
    reshape x3 -> x0, local copies, waits for them, and re-layouts: 6.35 us -> none  [the longest x1 2.41 us: fused_device(): queries.reshape(tokens, features)]
    pallas_call x1, Pallas kernels: 9.77 us -> 8.09 us  [fused_device(): pl.pallas_call(tail_kernel, out_shape=(jax.ShapeDtypeStruct(queries.shape...]
    unnamed x15 -> x16, local copies, waits for them, and re-layouts: 10.4 us -> 8.77 us
where the time goes in v2:
time: 76.9 us; the launch traced here: 76.5 us
  Pallas kernels  67.1 us (87%)
  local copies, waits for them, and re-layouts  8.77 us (11%)
    pallas_call x1, Pallas kernels, fused_device(): pl.pallas_call(functools.partial(learner_kernel, (n_tp, depth)), out_shap...  59 us
    unnamed x16, local copies, waits for them, and re-layouts  8.77 us
    pallas_call x1, Pallas kernels, fused_device(): pl.pallas_call(tail_kernel, out_shape=(jax.ShapeDtypeStruct(queries.shape...  8.09 us

profile of v2, /device:TPU:0, one launch (start us, length us, event | category | flops | bytes accessed | tf_op | source)
XLA Modules:
  0.0 76.5 jit_solution(16805167940688804000)
XLA Ops:
  0.6 0.0 copy-start
  0.6 1.6 %copy-done = bf16[1,2,2048,256]{3,2,1,0:T(8,128)(2,1)S(1)} copy-done((bf16[1,2,2048,256]{3,2,1,0:T(8,128)(2,1)S(1)}, bf16[1,2,2048,256]{3,2,1,0:T(8,128)(2,1)}, u32[]{:S(2)}) %copy-start) | copy-done | bytes 2097176
  2.2 0.0 copy-start.1
  2.2 1.6 %copy-done.1 = f32[2,1024,256]{2,1,0:T(8,128)S(1)} copy-done((f32[2,1024,256]{2,1,0:T(8,128)S(1)}, f32[2,1024,256]{2,1,0:T(8,128)}, u32[]{:S(2)}) %copy-start.1) | copy-done | bytes 2097176
  3.8 0.0 copy-start.2
  3.8 1.6 %copy-done.2 = f32[2,1024,256]{2,1,0:T(8,128)S(1)} copy-done((f32[2,1024,256]{2,1,0:T(8,128)S(1)}, f32[2,1024,256]{2,1,0:T(8,128)}, u32[]{:S(2)}) %copy-start.2) | copy-done | bytes 2097176
  5.4 0.0 copy-start.3
  5.4 1.6 %copy-done.3 = f32[2,1024,256]{2,1,0:T(8,128)S(1)} copy-done((f32[2,1024,256]{2,1,0:T(8,128)S(1)}, f32[2,1024,256]{2,1,0:T(8,128)}, u32[]{:S(2)}) %copy-start.3) | copy-done | bytes 2097176
  7.0 0.0 copy-start.4
  7.0 1.3 %copy-done.4 = bf16[48,24,2,256]{3,2,1,0:T(2,128)(2,1)S(1)} copy-done((bf16[48,24,2,256]{3,2,1,0:T(2,128)(2,1)S(1)}, bf16[48,24,2,256]{3,2,1,0:T(2,128)(2,1)}, u32[]{:S(2)}) %copy-start.4) | copy-done | bytes 1179672
  8.3 0.0 copy-start.5
  8.3 1.1 %copy-done.5 = bf16[48,4,2048]{2,1,0:T(4,128)(2,1)S(1)} copy-done((bf16[48,4,2048]{2,1,0:T(4,128)(2,1)S(1)}, bf16[48,4,2048]{2,1,0:T(4,128)(2,1)}, u32[]{:S(2)}) %copy-start.5) | copy-done | bytes 786456
  9.4 0.0 copy-start.6
  9.4 0.0 copy-start.7
  9.4 59.0 %shard_map.111 = (bf16[2,192,256]{2,1,0:T(8,128)(2,1)S(1)}, bf16[2,1152,256]{2,1,0:T(8,128)(2,1)S(1)}, f32[2,1024,256]{2,1,0:T(8,128)S(1)}, f32[2,1024,256]{2,1,0:T(8,128)S(1)}, f32[2,1024,256]{2,1,0:T(8,128)S(1)}) custom-call(bf16[1,2,2048,256]{3,2,1,0:T(8,128)(2,1)S(1)} %copy-done, f32[2,1024,256]{2,1,0:T(8,128)S(1)} %copy-done.1, ...), custom_call_target="tpu_custom_call" | custom-call | tf_op jit(solution)/shard_map/pallas_call | solution.py:377
  68.4 0.0 copy-done.6
  68.4 0.0 copy-done.7
  68.4 8.1 %shard_map.112 = (bf16[48,4,2048]{2,1,0:T(4,128)(2,1)}, f32[2,1024,256]{2,1,0:T(8,128)}, f32[2,1024,256]{2,1,0:T(8,128)}, f32[2,1024,256]{2,1,0:T(8,128)}) custom-call(s32[48]{0:T(128)S(1)} %copy-done.7, bf16[48,4,2048]{2,1,0:T(4,128)(2,1)S(1)} %copy-done.6, bf16[2,1152,256]{2,1,0:T(8,128)(2,1)S(1)} %get-tuple-element.13.kv_ref, ...), custom_call_target="tpu_custom_call" | custom-call | tf_op jit(solution)/shard_map/pallas_call | solution.py:419
Async XLA Ops:
  0.6 1.6 %copy-start = (bf16[1,2,2048,256]{3,2,1,0:T(8,128)(2,1)S(1)}, bf16[1,2,2048,256]{3,2,1,0:T(8,128)(2,1)}, u32[]{:S(2)}) copy-start(bf16[1,2,2048,256]{3,2,1,0:T(8,128)(2,1)} %grad_hbm.1) | copy-start | bytes 6291460
  2.2 1.6 %copy-start.1 = (f32[2,1024,256]{2,1,0:T(8,128)S(1)}, f32[2,1024,256]{2,1,0:T(8,128)}, u32[]{:S(2)}) copy-start(f32[2,1024,256]{2,1,0:T(8,128)} %master_hbm.1) | copy-start | bytes 6291460
  3.8 1.6 %copy-start.2 = (f32[2,1024,256]{2,1,0:T(8,128)S(1)}, f32[2,1024,256]{2,1,0:T(8,128)}, u32[]{:S(2)}) copy-start(f32[2,1024,256]{2,1,0:T(8,128)} %one_hbm.1) | copy-start | bytes 6291460
  5.4 1.6 %copy-start.3 = (f32[2,1024,256]{2,1,0:T(8,128)S(1)}, f32[2,1024,256]{2,1,0:T(8,128)}, u32[]{:S(2)}) copy-start(f32[2,1024,256]{2,1,0:T(8,128)} %two_hbm.1) | copy-start | bytes 6291460
  7.0 1.3 %copy-start.4 = (bf16[48,24,2,256]{3,2,1,0:T(2,128)(2,1)S(1)}, bf16[48,24,2,256]{3,2,1,0:T(2,128)(2,1)}, u32[]{:S(2)}) copy-start(bf16[48,24,2,256]{3,2,1,0:T(2,128)(2,1)} %kv_hbm.1) | copy-start | bytes 3538948
  8.3 1.1 %copy-start.5 = (bf16[48,4,2048]{2,1,0:T(4,128)(2,1)S(1)}, bf16[48,4,2048]{2,1,0:T(4,128)(2,1)}, u32[]{:S(2)}) copy-start(bf16[48,4,2048]{2,1,0:T(4,128)(2,1)} %x_hbm.1) | copy-start | bytes 2359300
  9.4 59.0 %copy-start.6 = (bf16[48,4,2048]{2,1,0:T(4,128)(2,1)S(1)}, bf16[48,4,2048]{2,1,0:T(4,128)(2,1)}, u32[]{:S(2)}) copy-start(bf16[48,4,2048]{2,1,0:T(4,128)(2,1)} %q_ref.1) | copy-start | bytes 2359300
  9.4 59.0 %copy-start.7 = (s32[48]{0:T(128)S(1)}, s32[48]{0:T(128)}, u32[]{:S(2)}) copy-start(s32[48]{0:T(128)} %lengths.1) | copy-start | bytes 580

commit v3 on v2

--- a/solution.py
+++ b/solution.py
@@ -374,6 +374,10 @@
     state = jax.ShapeDtypeStruct(master_weight.shape, f32)
     any_spec = pl.BlockSpec(memory_space=pl.ANY)
     hbm_spec = pl.BlockSpec(memory_space=pltpu.HBM)
+    in_place = [
+        pltpu.with_memory_space_constraint(array, pltpu.HBM)
+        for array in (grad_parts, master_weight, moment_one, moment_two, layer_inputs, kv_cache)
+    ]
     fresh, cached, master, one, two = pl.pallas_call(
         functools.partial(learner_kernel, (n_tp, depth)),
         out_shape=(
@@ -414,7 +418,7 @@
         compiler_params=pltpu.CompilerParams(
             collective_id=0, has_side_effects=True, vmem_limit_bytes=36 * 1024 * 1024
         ),
-    )(grad_parts, master_weight, moment_one, moment_two, layer_inputs, kv_cache)
+    )(*in_place)
     token_spec = pl.BlockSpec((TAIL_ROWS, step_count, features), lambda i, *_: (i, 0, 0))
     context, master, one, two = pl.pallas_call(
         tail_kernel,

time: 76.9 us -> 67.5 us (0.88)
  local copies, waits for them, and re-layouts: 8.77 us -> 0.01 us
    unnamed x16 -> x4, local copies, waits for them, and re-layouts: 8.77 us -> 0.01 us
where the time goes in v3:
time: 67.5 us; the launch traced here: 67.3 us
  Pallas kernels  66.6 us (99%)
    pallas_call x1, Pallas kernels, fused_device(): pl.pallas_call(functools.partial(learner_kernel, (n_tp, depth)), out_shap...  58.6 us
    pallas_call x1, Pallas kernels, fused_device(): pl.pallas_call(tail_kernel, out_shape=(jax.ShapeDtypeStruct(queries.shape...  8.09 us

profile of v3, /device:TPU:0, one launch (start us, length us, event | category | flops | bytes accessed | tf_op | source)
XLA Modules:
  0.0 67.3 jit_solution(14351051137894625083)
XLA Ops:
  0.6 0.0 copy-start.1
  0.6 0.0 copy-start
  0.7 58.6 %shard_map.111 = (bf16[2,192,256]{2,1,0:T(8,128)(2,1)S(1)}, bf16[2,1152,256]{2,1,0:T(8,128)(2,1)S(1)}, f32[2,1024,256]{2,1,0:T(8,128)S(1)}, f32[2,1024,256]{2,1,0:T(8,128)S(1)}, f32[2,1024,256]{2,1,0:T(8,128)S(1)}) custom-call(bf16[1,2,2048,256]{3,2,1,0:T(8,128)(2,1)} %grad_hbm.1, f32[2,1024,256]{2,1,0:T(8,128)} %master_hbm.1, f32[2,1024,256]{2,1,0:T(8,128)} %one_hbm.1, ...), custom_call_target="tpu_custom_call" | custom-call | tf_op jit(solution)/shard_map/pallas_call | solution.py:381
  59.2 0.0 copy-done.1
  59.2 0.0 copy-done
  59.2 8.1 %shard_map.112 = (bf16[48,4,2048]{2,1,0:T(4,128)(2,1)}, f32[2,1024,256]{2,1,0:T(8,128)}, f32[2,1024,256]{2,1,0:T(8,128)}, f32[2,1024,256]{2,1,0:T(8,128)}) custom-call(s32[48]{0:T(128)S(1)} %copy-done.1, bf16[48,4,2048]{2,1,0:T(4,128)(2,1)S(1)} %copy-done, bf16[2,1152,256]{2,1,0:T(8,128)(2,1)S(1)} %get-tuple-element.13.kv_ref, ...), custom_call_target="tpu_custom_call" | custom-call | tf_op jit(solution)/shard_map/pallas_call | solution.py:423
Async XLA Ops:
  0.6 58.6 %copy-start.1 = (s32[48]{0:T(128)S(1)}, s32[48]{0:T(128)}, u32[]{:S(2)}) copy-start(s32[48]{0:T(128)} %lengths.1) | copy-start | bytes 580
  0.6 58.6 %copy-start = (bf16[48,4,2048]{2,1,0:T(4,128)(2,1)S(1)}, bf16[48,4,2048]{2,1,0:T(4,128)(2,1)}, u32[]{:S(2)}) copy-start(bf16[48,4,2048]{2,1,0:T(4,128)(2,1)} %q_ref.1) | copy-start | bytes 2359300

commit v4 on v3

--- a/solution.py
+++ b/solution.py
@@ -170,22 +170,38 @@
     local[4].wait()
     local[5].wait()
 
-    def x_step(k, th):
+    ends_up, ends_down = t + 1 == n_tp - 1, t == 1
+
+    def x_wait(k, th):
         @pl.when(t - k >= 0)
         def _():
             x_arrived(t - k, th)
 
-            @pl.when(t < n_tp - 1)
-            def _():
-                x_move(t - k, th, 1).start()
-
         @pl.when(t + k < n_tp)
         def _():
             x_arrived(t + k, th)
 
-            @pl.when(t > 0)
-            def _():
-                x_move(t + k, th, 0).start()
+    def x_forward(k, th, go_up, go_down):
+        @pl.when((t - k >= 0) & (t < n_tp - 1) & go_up)
+        def _():
+            x_move(t - k, th, 1).start()
+
+        @pl.when((t + k < n_tp) & (t > 0) & go_down)
+        def _():
+            x_move(t + k, th, 0).start()
+
+    def x_first_half():
+        x_wait(1, f)
+        x_forward(1, f, ends_up, ends_down)
+
+    def x_second_half():
+        x_wait(1, nf)
+        x_forward(1, nf, True, True)
+        x_forward(1, f, jnp.logical_not(ends_up), jnp.logical_not(ends_down))
+
+    def x_far(k, th):
+        x_wait(k, th)
+        x_forward(k, th, True, True)
 
     def w_step(c):
         w_arrived(rx, c)
@@ -206,19 +222,19 @@
         lax.fori_loop(0, pieces, body, 0)
 
     split_cache(0)
-    x_step(1, f)
+    x_first_half()
     split_cache(1)
     w_step(0)
     split_cache(2)
-    x_step(1, nf)
+    x_second_half()
     split_cache(3)
     cached_copy = pltpu.make_async_copy(kv_flat, cached_out, out_sem.at[3])
     cached_copy.start()
     w_step(1)
     w_step(2)
-    x_step(2, f)
+    x_far(2, nf)
     w_step(3)
-    x_step(2, nf)
+    x_far(2, f)
 
     acc[...] = jnp.zeros_like(acc)
 
@@ -245,7 +261,7 @@
 
     def step(j, carry):
         k = j // 2
-        th = f + lax.rem(j, 2) * (1 - 2 * f)
+        th = nf + lax.rem(j, 2) * (1 - 2 * nf)
 
         def side(s, inner):
             z = t + (2 * s - 1) * k
@@ -263,10 +279,11 @@
         lax.fori_loop(jnp.where(k == 0, 1, 0), 2, side, 0)
         return carry
 
-    lax.fori_loop(0, 2 * n_tp, step, 0)
+    lax.fori_loop(0, 2 * n_tp - 1, step, 0)
 
     swap = remote(acc.at[nf], partner_acc, acc_send.at[0], acc_recv.at[0], partner)
     swap.start()
+    step(2 * n_tp - 1, 0)
     for c in range(W_CHUNKS):
         grad_copy(c).wait_send()
         w_copy(c, 0).wait_send()

time: 67.5 us -> 66.2 us (0.981)
  Pallas kernels: 66.6 us -> 65.4 us
    pallas_call x1, Pallas kernels: 58.6 us -> 57.3 us  [fused_device(): pl.pallas_call(functools.partial(learner_kernel, (n_tp, depth)), out_shap...]
where the time goes in v4:
time: 66.2 us; the launch traced here: 66 us
  Pallas kernels  65.4 us (99%)
  between operations  0.67 us (1%)
    pallas_call x1, Pallas kernels, fused_device(): pl.pallas_call(functools.partial(learner_kernel, (n_tp, depth)), out_shap...  57.3 us
    pallas_call x1, Pallas kernels, fused_device(): pl.pallas_call(tail_kernel, out_shape=(jax.ShapeDtypeStruct(queries.shape...  8.09 us

profile of v4, /device:TPU:0, one launch (start us, length us, event | category | flops | bytes accessed | tf_op | source)
XLA Modules:
  0.0 66.0 jit_solution(16212290170083697158)
XLA Ops:
  0.6 0.0 copy-start.1
  0.6 0.0 copy-start
  0.7 57.3 %shard_map.111 = (bf16[2,192,256]{2,1,0:T(8,128)(2,1)S(1)}, bf16[2,1152,256]{2,1,0:T(8,128)(2,1)S(1)}, f32[2,1024,256]{2,1,0:T(8,128)S(1)}, f32[2,1024,256]{2,1,0:T(8,128)S(1)}, f32[2,1024,256]{2,1,0:T(8,128)S(1)}) custom-call(bf16[1,2,2048,256]{3,2,1,0:T(8,128)(2,1)} %grad_hbm.1, f32[2,1024,256]{2,1,0:T(8,128)} %master_hbm.1, f32[2,1024,256]{2,1,0:T(8,128)} %one_hbm.1, ...), custom_call_target="tpu_custom_call" | custom-call | tf_op jit(solution)/shard_map/pallas_call | solution.py:398
  57.9 0.0 copy-done.1
  57.9 0.0 copy-done
  58.0 8.1 %shard_map.112 = (bf16[48,4,2048]{2,1,0:T(4,128)(2,1)}, f32[2,1024,256]{2,1,0:T(8,128)}, f32[2,1024,256]{2,1,0:T(8,128)}, f32[2,1024,256]{2,1,0:T(8,128)}) custom-call(s32[48]{0:T(128)S(1)} %copy-done.1, bf16[48,4,2048]{2,1,0:T(4,128)(2,1)S(1)} %copy-done, bf16[2,1152,256]{2,1,0:T(8,128)(2,1)S(1)} %get-tuple-element.13.kv_ref, ...), custom_call_target="tpu_custom_call" | custom-call | tf_op jit(solution)/shard_map/pallas_call | solution.py:440
Async XLA Ops:
  0.6 57.3 %copy-start.1 = (s32[48]{0:T(128)S(1)}, s32[48]{0:T(128)}, u32[]{:S(2)}) copy-start(s32[48]{0:T(128)} %lengths.1) | copy-start | bytes 580
  0.6 57.3 %copy-start = (bf16[48,4,2048]{2,1,0:T(4,128)(2,1)S(1)}, bf16[48,4,2048]{2,1,0:T(4,128)(2,1)}, u32[]{:S(2)}) copy-start(bf16[48,4,2048]{2,1,0:T(4,128)(2,1)} %q_ref.1) | copy-start | bytes 2359300

commit v5 on v4

--- a/solution.py
+++ b/solution.py
@@ -12,6 +12,8 @@
 W_CHUNKS = 4
 ADAM_SUB = 32
 TAIL_ROWS = 8
+TAIL_BLOCKS = 3
+LOG2E = 1.4426950408889634
 
 
 def learner_kernel(
@@ -328,51 +330,60 @@
             move.start()
         fresh_copy.wait()
 
-    row_count, step_count, features = q_ref.shape
-    cached = kv_ref.shape[1]
+    step_rows, step_count, features = q_ref.shape
+    row_count = TAIL_ROWS
     head = HD
-    cache_len = cached // row_count
+    cache_len = kv_ref.shape[1] // step_rows
+    cached = row_count * cache_len
     tokens = row_count * step_count
     keys = cached + tokens
     groups = fresh_ref.shape[2] // head
     per_group = features // head // groups
-    here = pl.ds(pl.multiple_of(block * tokens, tokens), tokens)
     column = lax.broadcasted_iota(jnp.int32, (1, keys), 1)
     is_old = column < cached
     new_column = column - cached
     key_row = jnp.where(is_old, column // cache_len, new_column // step_count)
     position = column - key_row * cache_len
-    limit = jnp.zeros((1, keys), jnp.int32)
-    for row in range(row_count):
-        limit = jnp.where(key_row == row, lengths[block * row_count + row], limit)
-    old_row = jnp.where(is_old & (position < limit), key_row, -1)
     new_row = jnp.where(is_old, -1, key_row)
     token = lax.broadcasted_iota(jnp.int32, (tokens, 1), 0)
     row = token // step_count
-    valid = (old_row == row) | ((new_row == row) & (new_column <= token))
+    new_valid = (new_row == row) & (new_column <= token)
     low = -0.7 * float(jnp.finfo(jnp.float32).max)
+    factor = head**-0.5 * LOG2E
     contract = (((1,), (1,)), ((), ()))
-    for group in range(groups):
-        cols = slice(group * head, (group + 1) * head)
-        query = jnp.concatenate(
-            [
-                q_ref[:, :, (group * per_group + h) * head : (group * per_group + h + 1) * head].reshape(tokens, head)
-                for h in range(per_group)
-            ],
-            axis=0,
-        )
-        key = jnp.concatenate([kv_ref[0, :, cols], fresh_ref[0, here, cols]], axis=0)
-        value = jnp.concatenate([kv_ref[1, :, cols], fresh_ref[1, here, cols]], axis=0)
-        scores = lax.dot_general(query, key, contract, preferred_element_type=jnp.float32)
-        scores = jnp.where(valid[None], scores.reshape(per_group, tokens, keys) * head**-0.5, low)
-        weights = jnp.exp(scores - jnp.max(scores, axis=-1, keepdims=True))
-        weights = weights * (1.0 / jnp.sum(weights, axis=-1, keepdims=True))
-        weights = weights.astype(jnp.bfloat16).reshape(per_group * tokens, keys)
-        out = jnp.dot(weights, value, preferred_element_type=jnp.float32)
-        for h in range(per_group):
-            at = (group * per_group + h) * head
-            piece = out[h * tokens : (h + 1) * tokens].reshape(row_count, step_count, head)
-            context[:, :, at : at + head] = piece.astype(jnp.bfloat16)
+    for part in range(step_rows // row_count):
+        first_row = part * row_count
+        start = block * step_rows + first_row
+        limit = jnp.zeros((1, keys), jnp.int32)
+        for at in range(row_count):
+            limit = jnp.where(key_row == at, lengths[start + at], limit)
+        valid = (jnp.where(is_old & (position < limit), key_row, -1) == row) | new_valid
+        here = pl.ds(pl.multiple_of(start * step_count, tokens), tokens)
+        old = slice(first_row * cache_len, first_row * cache_len + cached)
+        mine = slice(first_row, first_row + row_count)
+        for group in range(groups):
+            cols = slice(group * head, (group + 1) * head)
+            query = jnp.concatenate(
+                [
+                    q_ref[mine, :, (group * per_group + h) * head : (group * per_group + h + 1) * head].reshape(
+                        tokens, head
+                    )
+                    for h in range(per_group)
+                ],
+                axis=0,
+            )
+            key = jnp.concatenate([kv_ref[0, old, cols], fresh_ref[0, here, cols]], axis=0)
+            value = jnp.concatenate([kv_ref[1, old, cols], fresh_ref[1, here, cols]], axis=0)
+            scores = lax.dot_general(query, key, contract, preferred_element_type=jnp.float32)
+            scores = jnp.where(valid[None], scores.reshape(per_group, tokens, keys), low)
+            weights = jnp.exp2((scores - jnp.max(scores, axis=-1, keepdims=True)) * factor)
+            weights = weights * (1.0 / jnp.sum(weights, axis=-1, keepdims=True))
+            weights = weights.astype(jnp.bfloat16).reshape(per_group * tokens, keys)
+            out = jnp.dot(weights, value, preferred_element_type=jnp.float32)
+            for h in range(per_group):
+                at = (group * per_group + h) * head
+                piece = out[h * tokens : (h + 1) * tokens].reshape(row_count, step_count, head)
+                context[mine, :, at : at + head] = piece.astype(jnp.bfloat16)
 
     @pl.when(block == pl.num_programs(0) - 1)
     def _():
@@ -436,16 +447,17 @@
             collective_id=0, has_side_effects=True, vmem_limit_bytes=36 * 1024 * 1024
         ),
     )(*in_place)
-    token_spec = pl.BlockSpec((TAIL_ROWS, step_count, features), lambda i, *_: (i, 0, 0))
+    step_rows = TAIL_ROWS * TAIL_BLOCKS
+    token_spec = pl.BlockSpec((step_rows, step_count, features), lambda i, *_: (i, 0, 0))
     context, master, one, two = pl.pallas_call(
         tail_kernel,
         out_shape=(jax.ShapeDtypeStruct(queries.shape, bf16), state, state, state),
         grid_spec=pltpu.PrefetchScalarGridSpec(
             num_scalar_prefetch=1,
-            grid=(row_count // TAIL_ROWS,),
+            grid=(row_count // step_rows,),
             in_specs=[
                 token_spec,
-                pl.BlockSpec((2, TAIL_ROWS * cache_len, width), lambda i, *_: (0, i, 0)),
+                pl.BlockSpec((2, step_rows * cache_len, width), lambda i, *_: (0, i, 0)),
                 any_spec,
                 any_spec,
                 any_spec,

time: 66.2 us -> 62.5 us (0.944)
  Pallas kernels: 65.4 us -> 61.7 us
    pallas_call x1, Pallas kernels: 8.09 us -> 4.42 us  [fused_device(): pl.pallas_call(tail_kernel, out_shape=(jax.ShapeDtypeStruct(queries.shape...]
where the time goes in v5:
time: 62.5 us; the launch traced here: 62.4 us
  Pallas kernels  61.7 us (99%)
  between operations  0.67 us (1%)
    pallas_call x1, Pallas kernels, fused_device(): pl.pallas_call(functools.partial(learner_kernel, (n_tp, depth)), out_shap...  57.3 us
    pallas_call x1, Pallas kernels, fused_device(): pl.pallas_call(tail_kernel, out_shape=(jax.ShapeDtypeStruct(queries.shape...  4.42 us

profile of v5, /device:TPU:0, one launch (start us, length us, event | category | flops | bytes accessed | tf_op | source)
XLA Modules:
  0.0 62.4 jit_solution(16555199446154157040)
XLA Ops:
  0.6 0.0 copy-start.1
  0.6 0.0 copy-start
  0.7 57.3 %shard_map.111 = (bf16[2,192,256]{2,1,0:T(8,128)(2,1)S(1)}, bf16[2,1152,256]{2,1,0:T(8,128)(2,1)S(1)}, f32[2,1024,256]{2,1,0:T(8,128)S(1)}, f32[2,1024,256]{2,1,0:T(8,128)S(1)}, f32[2,1024,256]{2,1,0:T(8,128)S(1)}) custom-call(bf16[1,2,2048,256]{3,2,1,0:T(8,128)(2,1)} %grad_hbm.1, f32[2,1024,256]{2,1,0:T(8,128)} %master_hbm.1, f32[2,1024,256]{2,1,0:T(8,128)} %one_hbm.1, ...), custom_call_target="tpu_custom_call" | custom-call | tf_op jit(solution)/shard_map/pallas_call | solution.py:409
  57.9 0.0 copy-done.1
  57.9 0.0 copy-done
  58.0 4.4 %shard_map.112 = (bf16[48,4,2048]{2,1,0:T(4,128)(2,1)}, f32[2,1024,256]{2,1,0:T(8,128)}, f32[2,1024,256]{2,1,0:T(8,128)}, f32[2,1024,256]{2,1,0:T(8,128)}) custom-call(s32[48]{0:T(128)S(1)} %copy-done.1, bf16[48,4,2048]{2,1,0:T(4,128)(2,1)S(1)} %copy-done, bf16[2,1152,256]{2,1,0:T(8,128)(2,1)S(1)} %get-tuple-element.13.kv_ref, ...), custom_call_target="tpu_custom_call" | custom-call | tf_op jit(solution)/shard_map/pallas_call | solution.py:452
Async XLA Ops:
  0.6 57.3 %copy-start.1 = (s32[48]{0:T(128)S(1)}, s32[48]{0:T(128)}, u32[]{:S(2)}) copy-start(s32[48]{0:T(128)} %lengths.1) | copy-start | bytes 580
  0.6 57.3 %copy-start = (bf16[48,4,2048]{2,1,0:T(4,128)(2,1)S(1)}, bf16[48,4,2048]{2,1,0:T(4,128)(2,1)}, u32[]{:S(2)}) copy-start(bf16[48,4,2048]{2,1,0:T(4,128)(2,1)} %q_ref.1) | copy-start | bytes 2359300

commit v6 on v5

--- a/solution.py
+++ b/solution.py
@@ -250,13 +250,13 @@
             xflat[at, :] = xbuf[z, th, pl.ds(i * x_part, x_part)].reshape(flat_part, depth)
             return carry
 
-        lax.fori_loop(0, 4, flatten, 0)
+        lax.fori_loop(0, 4, flatten, 0, unroll=True)
 
         def one_side(kv, carry):
             acc[th, kv] += jnp.dot(xflat[...], wbuf[z, kv], preferred_element_type=jnp.float32)
             return carry
 
-        lax.fori_loop(0, 2, one_side, 0)
+        lax.fori_loop(0, 2, one_side, 0, unroll=True)
 
     for c in range(W_CHUNKS):
         w_arrived(rd, c)

time: 62.5 us -> 62.3 us (level)
  no operation moved by 1% of the time
where the time goes in v6:
time: 62.3 us; the launch traced here: 62.1 us
  Pallas kernels  61.5 us (99%)
  between operations  0.67 us (1%)
    pallas_call x1, Pallas kernels, fused_device(): pl.pallas_call(functools.partial(learner_kernel, (n_tp, depth)), out_shap...  57 us
    pallas_call x1, Pallas kernels, fused_device(): pl.pallas_call(tail_kernel, out_shape=(jax.ShapeDtypeStruct(queries.shape...  4.42 us

profile of v6, /device:TPU:0, one launch (start us, length us, event | category | flops | bytes accessed | tf_op | source)
XLA Modules:
  0.0 62.1 jit_solution(6584884779032806878)
XLA Ops:
  0.6 0.0 copy-start.1
  0.6 0.0 copy-start
  0.7 57.0 %shard_map.111 = (bf16[2,192,256]{2,1,0:T(8,128)(2,1)S(1)}, bf16[2,1152,256]{2,1,0:T(8,128)(2,1)S(1)}, f32[2,1024,256]{2,1,0:T(8,128)S(1)}, f32[2,1024,256]{2,1,0:T(8,128)S(1)}, f32[2,1024,256]{2,1,0:T(8,128)S(1)}) custom-call(bf16[1,2,2048,256]{3,2,1,0:T(8,128)(2,1)} %grad_hbm.1, f32[2,1024,256]{2,1,0:T(8,128)} %master_hbm.1, f32[2,1024,256]{2,1,0:T(8,128)} %one_hbm.1, ...), custom_call_target="tpu_custom_call" | custom-call | tf_op jit(solution)/shard_map/pallas_call | solution.py:409
  57.7 0.0 copy-done.1
  57.7 0.0 copy-done
  57.7 4.4 %shard_map.112 = (bf16[48,4,2048]{2,1,0:T(4,128)(2,1)}, f32[2,1024,256]{2,1,0:T(8,128)}, f32[2,1024,256]{2,1,0:T(8,128)}, f32[2,1024,256]{2,1,0:T(8,128)}) custom-call(s32[48]{0:T(128)S(1)} %copy-done.1, bf16[48,4,2048]{2,1,0:T(4,128)(2,1)S(1)} %copy-done, bf16[2,1152,256]{2,1,0:T(8,128)(2,1)S(1)} %get-tuple-element.13.kv_ref, ...), custom_call_target="tpu_custom_call" | custom-call | tf_op jit(solution)/shard_map/pallas_call | solution.py:452
Async XLA Ops:
  0.6 57.1 %copy-start.1 = (s32[48]{0:T(128)S(1)}, s32[48]{0:T(128)}, u32[]{:S(2)}) copy-start(s32[48]{0:T(128)} %lengths.1) | copy-start | bytes 580
  0.6 57.1 %copy-start = (bf16[48,4,2048]{2,1,0:T(4,128)(2,1)S(1)}, bf16[48,4,2048]{2,1,0:T(4,128)(2,1)}, u32[]{:S(2)}) copy-start(bf16[48,4,2048]{2,1,0:T(4,128)(2,1)} %q_ref.1) | copy-start | bytes 2359300
